TPU v7x, 32 devices: a whole 2x2x4 slice. The times are simulated.
32 devices in a mesh: ctx: 8 (over z, x), tp: 4 (over y, core).
Axes of the slice: x: 2, y: 2, z: 4, core: 2. Of those that a mesh axis runs over, the one named last changes fastest.
Arguments:
- inputs: bfloat16 [2048, 3, 4096], P('ctx', None, 'tp'), may hold values from -6 to 6
- short_filter: float32 [3, 3, 4096], P(None, None, 'tp'), may hold values from -2.5 to 2.5
- long_filter: bfloat16 [256, 128], P('tp'), may hold values from -0.5 to 0.5
- out_weight: bfloat16 [4096, 4096], P('tp'), may hold values from -0.09375 to 0.09375
- out_cotangent: bfloat16 [2048, 4096], P('ctx'), may hold values from -6 to 6
Outputs:
- result: bfloat16 [2048, 4096], P('ctx')
- grad_inputs: bfloat16 [2048, 3, 4096], P('ctx', None, 'tp')
- grad_short: float32 [3, 3, 4096], P(None, None, 'tp')
- grad_long: float32 [256, 128], P('tp')
All inputs are finite; a program needn't handle non-finite values.
Results may differ from a plain program's by a relative error of at most 0.009.
Values may be sent and summed in bfloat16 or wider, within the bound.
No kernel may reach another device: no remote copies, remote signals or barrier semaphores. Data moves between devices by JAX's collectives and lax.ppermute only.
A program may use at most 128 MiB of HBM per device.

v0:
```python
import jax
import jax.numpy as jnp
from jax import lax
from jax.sharding import PartitionSpec as P


def shifted(value, axis, steps):
    count = lax.axis_size(axis)
    initial, last = (max(0, -steps), min(count, count - steps))
    return lax.ppermute(value, axis, [(source, source + steps) for source in range(initial, last)])


def short_conv(extended, taps, count):
    span = taps.shape[0]
    total = taps[0] * extended[span - 1 : span - 1 + count]
    for lag in range(1, span):
        total = total + taps[lag] * extended[span - 1 - lag : span - 1 - lag + count]
    return total


def tap_table(filt, forward):
    span = filt.shape[1]
    row_pos = jnp.arange(span)[:, None]
    col_pos = jnp.arange(2 * span)[None, :]
    offset = row_pos - col_pos + span if forward else col_pos - row_pos
    valid = (offset >= 0) & (offset < span)
    picked = filt[:, jnp.clip(offset, 0, span - 1)]
    return jnp.where(valid[None], picked, jnp.zeros((), filt.dtype))


def block_conv(table, extended, blocks, group):
    span = table.shape[1]
    chans = extended.shape[1]
    first = extended[: blocks * span].reshape(blocks, span, chans // group, group)
    second = extended[span : (blocks + 1) * span].reshape(blocks, span, chans // group, group)
    total = jnp.einsum(
        "gij,bjgc->bigc", table[:, :, :span], first, preferred_element_type=jnp.float32
    )
    total = total + jnp.einsum(
        "gij,bjgc->bigc", table[:, :, span:], second, preferred_element_type=jnp.float32
    )
    return total.reshape(blocks * span, chans)


def rounded_term(values):
    return lax.optimization_barrier(values.astype(jnp.bfloat16)).astype(jnp.float32)


def local(inputs, short_filter, long_filter, out_weight, out_cotangent):
    count = inputs.shape[0]
    chans = inputs.shape[2]
    groups = long_filter.shape[0]
    span = long_filter.shape[1]
    lags = short_filter.shape[0]
    group = chans // groups
    blocks = count // span
    tokens_all = count * lax.axis_size("ctx")
    signal = inputs.astype(jnp.float32)
    zero_rows = jnp.zeros((lags - 1, 3, chans), jnp.float32)
    local_feat = short_conv(jnp.concatenate([zero_rows, signal], axis=0), short_filter, count)
    tail_gated = (local_feat[count - (span - 1) :, 1] * local_feat[count - (span - 1) :, 2]).astype(
        jnp.bfloat16
    )
    tail_inputs = inputs[count - (lags - 1) :].reshape(3 * (lags - 1), chans)
    sent = jnp.concatenate([tail_gated, tail_inputs], axis=0)
    taken = shifted(sent, "ctx", 1)
    gated_rim = taken[: span - 1]
    input_rim = taken[span - 1 :].reshape(lags - 1, 3, chans).astype(jnp.float32)
    signal_ext = jnp.concatenate([input_rim, signal], axis=0)
    feat = short_conv(signal_ext, short_filter, count)
    query, keyed, valued = (feat[:, 0], feat[:, 1], feat[:, 2])
    gated = (keyed * valued).astype(jnp.bfloat16)
    gated_ext = jnp.concatenate([jnp.zeros((1, chans), jnp.bfloat16), gated_rim, gated], axis=0)
    forward_table = tap_table(long_filter, True)
    mixed = block_conv(forward_table, gated_ext, blocks, group)
    gate_out = (query * mixed).astype(jnp.bfloat16)
    partial_value = rounded_term(jnp.dot(gate_out, out_weight, preferred_element_type=jnp.float32))
    result = lax.psum(partial_value.astype(jnp.bfloat16), "tp")
    grad_gate = lax.dot_general(
        out_cotangent, out_weight, (((1,), (1,)), ((), ())), preferred_element_type=jnp.float32
    )
    grad_mixed = (grad_gate * query).astype(jnp.bfloat16)
    grad_query = grad_gate * mixed
    backward_table = tap_table(long_filter, False)
    head_gated = block_conv(backward_table, grad_mixed, 1, group)[: lags - 1]
    head_feat = jnp.stack(
        [grad_query[: lags - 1], head_gated * valued[: lags - 1], head_gated * keyed[: lags - 1]],
        axis=1,
    ).astype(jnp.bfloat16)
    sent_back = jnp.concatenate(
        [grad_mixed[: span - 1], head_feat.reshape(3 * (lags - 1), chans)], axis=0
    )
    taken_back = shifted(sent_back, "ctx", -1)
    mixed_rim = taken_back[: span - 1]
    feat_rim = taken_back[span - 1 :].reshape(lags - 1, 3, chans)
    mixed_ext = jnp.concatenate(
        [grad_mixed, mixed_rim, jnp.zeros((1, chans), jnp.bfloat16)], axis=0
    )
    grad_gated = block_conv(backward_table, mixed_ext, blocks, group)
    grad_feat = jnp.stack([grad_query, grad_gated * valued, grad_gated * keyed], axis=1).astype(
        jnp.bfloat16
    )
    grad_feat_ext = lax.optimization_barrier(jnp.concatenate([grad_feat, feat_rim], axis=0)).astype(
        jnp.float32
    )
    grad_in = short_filter[0] * grad_feat_ext[:count]
    for lag in range(1, lags):
        grad_in = grad_in + short_filter[lag] * grad_feat_ext[lag : lag + count]
    grad_feat32 = grad_feat_ext[:count]
    short_rows = [
        jnp.sum(grad_feat32 * signal_ext[lags - 1 - lag : lags - 1 - lag + count], axis=0)
        for lag in range(lags)
    ]
    short_local = jnp.stack(short_rows, axis=0)
    mixed_blocks = grad_mixed.reshape(blocks, span, groups, group)
    earlier = gated_ext[:count].reshape(blocks, span, groups, group)
    current = gated_ext[span:].reshape(blocks, span, groups, group)
    products = jnp.concatenate(
        [
            jnp.einsum("bigc,bjgc->gij", mixed_blocks, earlier, preferred_element_type=jnp.float32),
            jnp.einsum("bigc,bjgc->gij", mixed_blocks, current, preferred_element_type=jnp.float32),
        ],
        axis=2,
    )
    flipped = products[:, :, ::-1].reshape(groups, 2 * span * span)
    skewed = flipped[:, span - 1 : span - 1 + span * (2 * span - 1)].reshape(
        groups, span, 2 * span - 1
    )[:, :, :span]
    long_local = jnp.sum(skewed, axis=1)
    long_total, short_total = lax.psum((long_local, short_local), "ctx")
    grad_short = short_total * float(tokens_all) ** (-0.5)
    grad_long = long_total * float(tokens_all * group) ** (-0.5)
    return (result, grad_in.astype(jnp.bfloat16), grad_short, grad_long)


def solution(mesh):
    in_specs = (
        P("ctx", None, "tp"),
        P(None, None, "tp"),
        P("tp", None),
        P("tp", None),
        P("ctx", None),
    )
    out_specs = (P("ctx", None), P("ctx", None, "tp"), P(None, None, "tp"), P("tp", None))
    return jax.shard_map(local, mesh=mesh, in_specs=in_specs, out_specs=out_specs, check_vma=False)
```

profile of v0, /device:TPU:0, one launch (start us, length us, event | category | flops | bytes accessed | tf_op | source)
XLA Modules:
  0.0 584.0 jit_solution(4579067291675489319)
XLA Ops:
  7.2 3.6 convert_element_type.48
  10.8 0.8 slice.132
  11.7 5.0 multiply_add_fusion.1
  16.9 4.9 collective-permute-start
  22.1 115.0 %gather_fusion = bf16[32768,64]{1,0:T(8,128)(2,1)} fusion(bf16[64,128]{0,1:T(8,128)(2,1)S(1)} %copy.30, s32[32768]{0:T(1024)S(1)} %broadcast_clamp_fusion.1), kind=kCustom, calls=%fused_computation | custom fusion | bytes 8519680 | tf_op jit(solution)/shard_map/gather | solution.py:27
  137.1 10.1 %copy.63 = bf16[128,256,64]{1,0,2:T(8,128)(2,1)} copy(bf16[128,256,64]{2,1,0:T(8,128)(2,1)} %bitcast.111) | data formatting | bytes 8388608 | tf_op jit(solution)/shard_map/gather | solution.py:27
  147.3 115.0 %gather_fusion.1 = bf16[32768,64]{1,0:T(8,128)(2,1)} fusion(bf16[64,128]{0,1:T(8,128)(2,1)S(1)} %copy.30, s32[32768]{0:T(1024)S(1)} %broadcast_clamp_fusion), kind=kCustom, calls=%fused_computation.1 | custom fusion | bytes 8519680 | tf_op jit(solution)/shard_map/gather | solution.py:27
  262.3 10.1 %copy.64 = bf16[128,256,64]{1,0,2:T(8,128)(2,1)} copy(bf16[128,256,64]{2,1,0:T(8,128)(2,1)} %bitcast.110) | data formatting | bytes 8388608 | tf_op jit(solution)/shard_map/gather | solution.py:27
  272.4 4.6 select_bitcast_fusion.1
  276.9 2.2 select_bitcast_fusion
  279.2 5.0 multiply_add_fusion
  284.4 1.6 copy-done.3
  286.1 1.0 copy.33
  287.1 1.2 convert_element_type.55
  288.3 0.9 pad_maximum_fusion.5
  289.2 2.0 copy.29
  291.2 1.2 reshape.165
  292.4 3.0 fusion.4
  295.4 2.8 fusion.23
  298.2 0.6 copy.35
  298.7 1.0 copy.88
  299.8 2.5 copy.36
  302.3 7.1 %multiply_convert_fusion.3 = (bf16[256,1024]{1,0:T(8,128)(2,1)}, bf16[256,1024]{1,0:T(8,128)(2,1)S(1)}) fusion(f32[256,1024]{1,0:T(8,128)} %copy.36, f32[256,3,1024]{2,0,1:T(8,128)} %copy-done.3, bf16[256,4096]{1,0:T(8,128)(2,1)S(1)} %copy-done, bf16[1024,4096]{1,0:T(8,128)(2,1)} %param.8), kind=kOutput, calls=%fused_computation.49 | convolution fusion | flops 2148532224 | bytes 13631488 | tf_op jit(solution)/shard_map/dot_general | solution.py:79
  309.8 2.7 convolution_bitcast_fusion
  312.5 2.7 convolution_bitcast_fusion.1
  315.6 2.8 fusion.11
  318.4 2.8 fusion.27
  321.4 0.8 fusion.49
  322.3 1.3 collective-permute-start.1
  323.6 7.7 %pad_maximum_fusion = f32[64,128,256]{1,2,0:T(8,128)} fusion(f32[64,128,128]{1,2,0:T(8,128)} %convolution_bitcast_fusion, f32[64,128,128]{1,2,0:T(8,128)} %convolution_bitcast_fusion.1), kind=kLoop, calls=%fused_computation.2 | loop fusion | flops 2097152 | bytes 16777216 | tf_op jit(solution)/shard_map/concatenate | solution.py:118
  331.3 63.8 %rev.3 = f32[64,128,256]{1,2,0:T(8,128)} reverse(f32[64,128,256]{1,2,0:T(8,128)} %pad_maximum_fusion), dimensions={2} | reverse | bytes 16777216 | tf_op jit(solution)/shard_map/rev | solution.py:125
  395.2 9.2 %copy.69 = f32[8,8,128,256]{3,1,2,0:T(8,128)} copy(f32[8,8,128,256]{2,3,1,0:T(8,128)} %bitcast.108) | data formatting | bytes 16777216
  404.3 8.8 %slice.190 = f32[64,32640]{1,0:T(8,128)} slice(f32[64,32768]{1,0:T(8,128)} %bitcast.109), slice={[0:64], [127:32767]} | slice | bytes 16711680 | tf_op jit(solution)/shard_map/slice | solution.py:126
  413.2 15.9 %reshape.174 = f32[64,128,255]{2,1,0:T(8,128)} reshape(f32[64,32640]{1,0:T(8,128)} %slice.190) | data formatting | bytes 16711680 | tf_op jit(solution)/shard_map/reshape | solution.py:126
  429.1 3.3 slice_reduce_fusion
  432.9 2.8 fusion.6
  435.6 2.8 fusion.19
  439.0 0.8 reshape.171
  440.2 1.9 multiply_convert_fusion.1
  442.7 1.5 copy-done.2
  444.6 3.1 multiply_reduce_fusion.1
  447.7 0.6 pad_maximum_fusion.9
  448.4 7.4 %convolution_convert_fusion = bf16[256,4096]{1,0:T(8,128)(2,1)} fusion(bf16[1024,4096]{1,0:T(8,128)(2,1)} %param.8, f32[256,1024]{1,0:T(8,128)S(1)} %copy-done.8, f32[256,3,1024]{2,0,1:T(8,128)} %copy-done.3), kind=kOutput, calls=%fused_computation.3 | convolution fusion | flops 2149056512 | bytes 12582912 | tf_op jit(solution)/shard_map/dot_general | solution.py:77
  455.8 64.1 %all-reduce.7.cloned.1.call-done = (f32[3,3,1024]{2,1,0:T(4,128)}, f32[64,128]{1,0:T(8,128)}) async-done(((f32[3,3,1024]{2,1,0:T(4,128)}, f32[64,128]{1,0:T(8,128)}), (f32[3,3,1024]{2,1,0:T(4,128)}, f32[64,128]{1,0:T(8,128)})) %all-reduce.7.cloned.1.call-update) | async-done | bytes 69648 | tf_op jit(solution)/shard_map/psum | solution.py:130
  519.9 1.4 broadcast_multiply_fusion.1
  521.3 1.4 broadcast_multiply_fusion
  522.7 51.3 %all-reduce.5.cloned.1.call-done = bf16[256,4096]{1,0:T(8,128)(2,1)} async-done(((bf16[256,4096]{1,0:T(8,128)(2,1)}), bf16[256,4096]{1,0:T(8,128)(2,1)}) %all-reduce.5.cloned.1.call-update) | async-done | bytes 2097168 | tf_op jit(solution)/shard_map/psum | solution.py:78
  574.0 3.1 copy.92
  (72 shorter events, 4.5 us)
Async XLA Ops:
  7.2 295.1 %copy-start = (bf16[256,4096]{1,0:T(8,128)(2,1)S(1)}, bf16[256,4096]{1,0:T(8,128)(2,1)}, u32[]{:S(2)}) copy-start(bf16[256,4096]{1,0:T(8,128)(2,1)} %param.9) | copy-start | bytes 6291460
  7.2 4.5 copy-start.10
  7.2 512.7 %all-reduce.7.cloned.1.call-start = ((), (), s32[]{:S(2)}) async-start(), calls=%async_computation.1 | async-start | bytes 163840 | tf_op jit(solution)/shard_map/psum | solution.py:130
  11.7 10.2 %copy-start.11 = (bf16[64,128]{1,0:T(8,128)(2,1)S(1)}, bf16[64,128]{1,0:T(8,128)(2,1)}, u32[]{:S(2)}) copy-start(bf16[64,128]{1,0:T(8,128)(2,1)} %param.7) | copy-start | bytes 49156
  16.9 262.3 %collective-permute-start = (bf16[133,1024]{1,0:T(8,128)(2,1)S(1)}, bf16[133,1024]{1,0:T(8,128)(2,1)S(1)}, u32[]{:S(2)}, u32[]{:S(2)}) collective-permute-start(bf16[133,1024]{1,0:T(8,128)(2,1)S(1)} %pad_maximum_fusion.7), channel_id=1, source_target_pairs={{0,4},{4,8},{8,12},{12,16},{16,20},{20,24},{24,28},{1,5},{5,9},{9,... | collective-permute-start | bytes 817160 | tf_op jit(solution)/shard_map/ppermute | solution.py:10
  272.4 4.6 copy-start.4
  284.2 1.7 copy-start.3
  292.4 5.8 copy-start.6
  309.7 2.9 copy-start.7
  315.6 6.6 %copy-start.9 = (bf16[256,1024]{1,0:T(8,128)(2,1)S(1)}, bf16[256,1024]{1,0:T(8,128)(2,1)}, u32[]{:S(2)}) copy-start(bf16[256,1024]{1,0:T(8,128)(2,1)} %get-tuple-element.14) | copy-start | bytes 1572868
  322.3 110.0 %collective-permute-start.1 = (bf16[133,1024]{1,0:T(8,128)(2,1)S(1)}, bf16[133,1024]{1,0:T(8,128)(2,1)S(1)}, u32[]{:S(2)}, u32[]{:S(2)}) collective-permute-start(bf16[133,1024]{1,0:T(8,128)(2,1)S(1)} %pad_maximum_fusion.8), channel_id=1, source_target_pairs={{4,0},{8,4},{12,8},{16,12},{20,16},{24,20},{28,24},{5,1},{9,5},{13... | collective-permute-start | bytes 817160 | tf_op jit(solution)/shard_map/ppermute | solution.py:10
  442.2 1.9 copy-start.2
  442.3 2.3 copy-start.5
  444.6 3.8 copy-start.8
  448.4 125.7 %all-reduce.5.cloned.1.call-start = ((), (), s32[]{:S(2)}) async-start(), calls=%async_computation | async-start | bytes 4194304 | tf_op jit(solution)/shard_map/psum | solution.py:78
  455.8 121.3 %copy-start.1 = (bf16[256,4096]{1,0:T(8,128)(2,1)S(1)}, bf16[256,4096]{1,0:T(8,128)(2,1)}, u32[]{:S(2)}) copy-start(bf16[256,4096]{1,0:T(8,128)(2,1)} %param.9) | copy-start | bytes 6291460
Sparse Core Ops, SparseCore 0:
  448.5 71.3 all-reduce.6
  522.8 51.1 all-reduce.4
where the time goes:
time: 590 us; the launch traced here: 584 us
  local copies, waits for them, and re-layouts  368 us (62%)
  waiting for transfers between devices  115 us (19%)
  other arithmetic  42.7 us (7%)
  matrix products  36.9 us (6%)
  between operations  14.5 us (2%)
  starting transfers between devices  6.23 us (1%)
    gather x4, local copies, waits for them, and re-layouts, tap_table(): picked = filt[:, jnp.clip(offset, 0, span - 1)]  250 us
    psum x1, waiting for transfers between devices, local(): long_total, short_total = lax.psum((long_local, short_local), 'ctx')  64.1 us
    rev x1, local copies, waits for them, and re-layouts, local(): flipped = products[:, :, ::-1].reshape(groups, 2 * span * span)  63.8 us
    psum x1, waiting for transfers between devices, local(): result = lax.psum(partial_value.astype(jnp.bfloat16), 'tp')  51.3 us
    unnamed x30, local copies, waits for them, and re-layouts  17.1 us
    reshape x1, local copies, waits for them, and re-layouts, local(): flipped[:, span - 1:span - 1 + span * (2 * span - 1)]  15.9 us
  transfers between devices with their start and end apart: 4, of which 2 were waited for; matrix products, arithmetic and copies ran while one was open for 64% of the time, Pallas kernels for 0%

commit v1 on v0

--- a/solution.py
+++ b/solution.py
@@ -75,7 +75,12 @@
     mixed = block_conv(forward_table, gated_ext, blocks, group)
     gate_out = (query * mixed).astype(jnp.bfloat16)
     partial_value = rounded_term(jnp.dot(gate_out, out_weight, preferred_element_type=jnp.float32))
-    result = lax.psum(partial_value.astype(jnp.bfloat16), "tp")
+
+    def close_block(chunk):
+        outer = jnp.sum(lax.all_gather(chunk, "tp"), 0)
+        return outer
+
+    result = close_block(partial_value.astype(jnp.bfloat16))
     grad_gate = lax.dot_general(
         out_cotangent, out_weight, (((1,), (1,)), ((), ())), preferred_element_type=jnp.float32
     )

time: 590 us -> 544 us (0.922)
  waiting for transfers between devices: 115 us -> 63.8 us
  other arithmetic: 42.7 us -> 49.7 us
    psum x1 -> x0, waiting for transfers between devices: 51.3 us -> none  [local(): result = lax.psum(partial_value.astype(jnp.bfloat16), 'tp')]
    reduce_sum x0 -> x1, other arithmetic: none -> 7.03 us  [close_block(): outer = jnp.sum(lax.all_gather(chunk, 'tp'), 0)]
    unnamed x30 -> x29, local copies, waits for them, and re-layouts: 17.1 us -> 14 us
  transfers between devices with their start and end apart: 4 -> 4, of which waited for: 2 -> 1; matrix products, arithmetic and copies ran while one was open for 64% -> 70% of each run, Pallas kernels for 0% -> 0%
where the time goes in v1:
time: 544 us; the launch traced here: 538 us
  local copies, waits for them, and re-layouts  365 us (67%)
  waiting for transfers between devices  63.8 us (12%)
  other arithmetic  49.7 us (9%)
  matrix products  36.9 us (7%)
  between operations  15.9 us (3%)
  starting transfers between devices  6.49 us (1%)
    gather x4, local copies, waits for them, and re-layouts, tap_table(): picked = filt[:, jnp.clip(offset, 0, span - 1)]  250 us
    rev x1, local copies, waits for them, and re-layouts, local(): flipped = products[:, :, ::-1].reshape(groups, 2 * span * span)  63.8 us
    psum x1, waiting for transfers between devices, local(): long_total, short_total = lax.psum((long_local, short_local), 'ctx')  63.8 us
    reshape x1, local copies, waits for them, and re-layouts, local(): flipped[:, span - 1:span - 1 + span * (2 * span - 1)]  15.9 us
    unnamed x29, local copies, waits for them, and re-layouts  14 us
  transfers between devices with their start and end apart: 4, of which 1 were waited for; matrix products, arithmetic and copies ran while one was open for 70% of the time, Pallas kernels for 0%

profile of v1, /device:TPU:0, one launch (start us, length us, event | category | flops | bytes accessed | tf_op | source)
XLA Modules:
  0.0 538.0 jit_solution(17421245676644211805)
XLA Ops:
  8.1 3.6 convert_element_type.50
  11.7 0.8 slice.132
  12.6 5.0 multiply_add_fusion.1
  17.7 4.9 collective-permute-start
  23.0 115.0 %gather_fusion = bf16[32768,64]{1,0:T(8,128)(2,1)} fusion(bf16[64,128]{0,1:T(8,128)(2,1)S(1)} %copy.30, s32[32768]{0:T(1024)S(1)} %broadcast_clamp_fusion.1), kind=kCustom, calls=%fused_computation | custom fusion | bytes 8519680 | tf_op jit(solution)/shard_map/gather | solution.py:27
  138.0 10.1 %copy.63 = bf16[128,256,64]{1,0,2:T(8,128)(2,1)} copy(bf16[128,256,64]{2,1,0:T(8,128)(2,1)} %bitcast.112) | data formatting | bytes 8388608 | tf_op jit(solution)/shard_map/gather | solution.py:27
  148.1 115.0 %gather_fusion.1 = bf16[32768,64]{1,0:T(8,128)(2,1)} fusion(bf16[64,128]{0,1:T(8,128)(2,1)S(1)} %copy.30, s32[32768]{0:T(1024)S(1)} %broadcast_clamp_fusion), kind=kCustom, calls=%fused_computation.1 | custom fusion | bytes 8519680 | tf_op jit(solution)/shard_map/gather | solution.py:27
  263.1 10.1 %copy.64 = bf16[128,256,64]{1,0,2:T(8,128)(2,1)} copy(bf16[128,256,64]{2,1,0:T(8,128)(2,1)} %bitcast.111) | data formatting | bytes 8388608 | tf_op jit(solution)/shard_map/gather | solution.py:27
  273.2 4.6 select_bitcast_fusion.1
  277.8 2.2 select_bitcast_fusion
  280.1 5.0 multiply_add_fusion
  285.2 1.6 copy-done.3
  286.9 1.0 copy.33
  287.9 1.2 convert_element_type.57
  289.1 0.9 pad_maximum_fusion.5
  290.0 2.0 copy.29
  292.0 1.2 reshape.165
  293.2 3.0 fusion.4
  296.2 2.8 fusion.23
  299.0 0.6 copy.35
  299.5 1.0 copy.88
  300.6 2.5 copy.36
  303.1 7.1 %multiply_convert_fusion.3 = (bf16[256,1024]{1,0:T(8,128)(2,1)}, bf16[256,1024]{1,0:T(8,128)(2,1)S(1)}) fusion(f32[256,1024]{1,0:T(8,128)} %copy.36, f32[256,3,1024]{2,0,1:T(8,128)} %copy-done.3, bf16[256,4096]{1,0:T(8,128)(2,1)S(1)} %copy-done, bf16[1024,4096]{1,0:T(8,128)(2,1)} %param.8), kind=kOutput, calls=%fused_computation.49 | convolution fusion | flops 2148532224 | bytes 13631488 | tf_op jit(solution)/shard_map/dot_general | solution.py:84
  310.6 2.7 convolution_bitcast_fusion
  313.4 2.7 convolution_bitcast_fusion.1
  316.4 2.8 fusion.11
  319.2 2.8 fusion.27
  322.3 0.8 fusion.49
  323.2 1.3 collective-permute-start.1
  324.5 7.7 %pad_maximum_fusion = f32[64,128,256]{1,2,0:T(8,128)} fusion(f32[64,128,128]{1,2,0:T(8,128)} %convolution_bitcast_fusion, f32[64,128,128]{1,2,0:T(8,128)} %convolution_bitcast_fusion.1), kind=kLoop, calls=%fused_computation.2 | loop fusion | flops 2097152 | bytes 16777216 | tf_op jit(solution)/shard_map/concatenate | solution.py:123
  332.2 63.8 %rev.3 = f32[64,128,256]{1,2,0:T(8,128)} reverse(f32[64,128,256]{1,2,0:T(8,128)} %pad_maximum_fusion), dimensions={2} | reverse | bytes 16777216 | tf_op jit(solution)/shard_map/rev | solution.py:130
  396.0 9.2 %copy.69 = f32[8,8,128,256]{3,1,2,0:T(8,128)} copy(f32[8,8,128,256]{2,3,1,0:T(8,128)} %bitcast.109) | data formatting | bytes 16777216
  405.2 8.8 %slice.190 = f32[64,32640]{1,0:T(8,128)} slice(f32[64,32768]{1,0:T(8,128)} %bitcast.110), slice={[0:64], [127:32767]} | slice | bytes 16711680 | tf_op jit(solution)/shard_map/slice | solution.py:131
  414.0 15.9 %reshape.174 = f32[64,128,255]{2,1,0:T(8,128)} reshape(f32[64,32640]{1,0:T(8,128)} %slice.190) | data formatting | bytes 16711680 | tf_op jit(solution)/shard_map/reshape | solution.py:131
  429.9 3.3 slice_reduce_fusion
  433.7 2.8 fusion.6
  436.5 2.8 fusion.19
  439.3 0.6 copy.48
  439.8 0.8 reshape.171
  441.0 1.9 multiply_convert_fusion.1
  443.5 1.5 copy-done.2
  445.4 3.1 multiply_reduce_fusion.1
  448.5 0.6 pad_maximum_fusion.9
  449.5 7.4 %convolution_convert_fusion = bf16[256,4096]{1,0:T(8,128)(2,1)} fusion(bf16[1024,4096]{1,0:T(8,128)(2,1)} %param.8, f32[256,1024]{1,0:T(8,128)S(1)} %copy-done.8, f32[256,3,1024]{2,0,1:T(8,128)} %copy-done.3), kind=kOutput, calls=%fused_computation.3 | convolution fusion | flops 2149056512 | bytes 12582912 | tf_op jit(solution)/shard_map/dot_general | solution.py:77
  456.9 63.8 %all-reduce.4.cloned.1.call-done = (f32[3,3,1024]{2,1,0:T(4,128)}, f32[64,128]{1,0:T(8,128)}) async-done(((f32[3,3,1024]{2,1,0:T(4,128)}, f32[64,128]{1,0:T(8,128)}), (f32[3,3,1024]{2,1,0:T(4,128)}, f32[64,128]{1,0:T(8,128)})) %all-reduce.4.cloned.1.call-update) | async-done | bytes 69648 | tf_op jit(solution)/shard_map/psum | solution.py:135
  520.7 1.4 broadcast_multiply_fusion.1
  522.1 1.4 broadcast_multiply_fusion
  523.5 7.0 %reduce_sum.48 = bf16[256,4096]{1,0:T(8,128)(2,1)} reduce(bf16[4,256,4096]{2,1,0:T(8,128)(2,1)} %bitcast.113, bf16[]{:T(256)} %constant.8.clone.1), dimensions={0}, to_apply=%region_0.1 | reduce | flops 3145728 | bytes 10485762 | tf_op jit(solution)/shard_map/reduce_sum | solution.py:80
  (72 shorter events, 4.2 us)
Async XLA Ops:
  8.0 295.1 %copy-start = (bf16[256,4096]{1,0:T(8,128)(2,1)S(1)}, bf16[256,4096]{1,0:T(8,128)(2,1)}, u32[]{:S(2)}) copy-start(bf16[256,4096]{1,0:T(8,128)(2,1)} %param.9) | copy-start | bytes 6291460
  8.0 4.5 copy-start.10
  8.0 512.7 %all-reduce.4.cloned.1.call-start = ((), (), s32[]{:S(2)}) async-start(), calls=%async_computation.1 | async-start | bytes 163840 | tf_op jit(solution)/shard_map/psum | solution.py:135
  12.6 10.2 %copy-start.11 = (bf16[64,128]{1,0:T(8,128)(2,1)S(1)}, bf16[64,128]{1,0:T(8,128)(2,1)}, u32[]{:S(2)}) copy-start(bf16[64,128]{1,0:T(8,128)(2,1)} %param.7) | copy-start | bytes 49156
  17.7 262.3 %collective-permute-start = (bf16[133,1024]{1,0:T(8,128)(2,1)S(1)}, bf16[133,1024]{1,0:T(8,128)(2,1)S(1)}, u32[]{:S(2)}, u32[]{:S(2)}) collective-permute-start(bf16[133,1024]{1,0:T(8,128)(2,1)S(1)} %pad_maximum_fusion.7), channel_id=1, source_target_pairs={{0,4},{4,8},{8,12},{12,16},{16,20},{20,24},{24,28},{1,5},{5,9},{9,... | collective-permute-start | bytes 817160 | tf_op jit(solution)/shard_map/ppermute | solution.py:10
  273.2 4.6 copy-start.4
  285.1 1.7 copy-start.3
  293.2 5.8 %copy-start.6 = (bf16[2,128,64,16]{1,0,3,2:T(2,128)(2,1)}, bf16[2,128,64,16]{1,0,3,2:T(2,128)(2,1)S(1)}, u32[]{:S(2)}) copy-start(bf16[2,128,64,16]{1,0,3,2:T(2,128)(2,1)S(1)} %reshape.165) | copy-start | bytes 1572868
  310.5 2.9 copy-start.7
  316.4 6.6 %copy-start.9 = (bf16[256,1024]{1,0:T(8,128)(2,1)S(1)}, bf16[256,1024]{1,0:T(8,128)(2,1)}, u32[]{:S(2)}) copy-start(bf16[256,1024]{1,0:T(8,128)(2,1)} %get-tuple-element.14) | copy-start | bytes 1572868
  323.2 110.0 %collective-permute-start.1 = (bf16[133,1024]{1,0:T(8,128)(2,1)S(1)}, bf16[133,1024]{1,0:T(8,128)(2,1)S(1)}, u32[]{:S(2)}, u32[]{:S(2)}) collective-permute-start(bf16[133,1024]{1,0:T(8,128)(2,1)S(1)} %pad_maximum_fusion.8), channel_id=1, source_target_pairs={{4,0},{8,4},{12,8},{16,12},{20,16},{24,20},{28,24},{5,1},{9,5},{13... | collective-permute-start | bytes 817160 | tf_op jit(solution)/shard_map/ppermute | solution.py:10
  443.1 1.9 copy-start.2
  443.1 2.3 copy-start.5
  445.4 4.1 copy-start.8
  449.2 74.3 %all-gather.3.cloned.1.call-start = ((), (), s32[]{:S(2)}) async-start(), calls=%async_computation | async-start | bytes 10485760 | tf_op jit(solution)/shard_map/all_gather | solution.py:80
  523.5 7.0 %copy-start.1 = (bf16[256,4096]{1,0:T(8,128)(2,1)S(1)}, bf16[256,4096]{1,0:T(8,128)(2,1)}, u32[]{:S(2)}) copy-start(bf16[256,4096]{1,0:T(8,128)(2,1)} %param.9) | copy-start | bytes 6291460
Sparse Core Ops, SparseCore 0:
  449.3 71.3 all-reduce.3
Sparse Core Ops, SparseCore 1:
  457.0 60.5 all-gather.2
